TPU v7x, 32 devices: a whole 2x2x4 slice. The times are simulated.
32 devices in a mesh: fsdp: 8 (over z, y), ctx: 2 (over x), tp: 2 (over core).
Axes of the slice: x: 2, y: 2, z: 4, core: 2. Of those that a mesh axis runs over, the one named last changes fastest.
Arguments:
- tokens: bfloat16 [3584, 2304], P(('fsdp', 'ctx')), may hold values from -6 to 6
- cotangent: bfloat16 [3584, 2304], P(('fsdp', 'ctx')), may hold values from -6 to 6
- lengths: int32 [8, 1], P('fsdp'), may hold values from 224 to 448, as said below
- positions: int32 [8, 448], P('fsdp'), may hold values from 0 to 447, each once within a row
- query_weight: bfloat16 [2304, 2048], P('fsdp', 'tp'), may hold values from -0.5 to 0.5
- key_weight: bfloat16 [2304, 1024], P('fsdp', 'tp'), may hold values from -0.5 to 0.5
- value_weight: bfloat16 [2304, 1024], P('fsdp', 'tp'), may hold values from -0.125 to 0.125
- output_weight: bfloat16 [2048, 2304], P('tp', 'fsdp'), may hold values from -0.125 to 0.125
- gate_weight: bfloat16 [2304, 9216], P('fsdp', 'tp'), may hold values from -0.125 to 0.125
- up_weight: bfloat16 [2304, 9216], P('fsdp', 'tp'), may hold values from -0.125 to 0.125
- down_weight: bfloat16 [9216, 2304], P('tp', 'fsdp'), may hold values from -0.0625 to 0.0625
- gain_attn_in: bfloat16 [2304], P('fsdp'), may hold values from -0.5 to 0.5
- gain_attn_out: bfloat16 [2304], P('fsdp'), may hold values from -0.5 to 0.5
- gain_ffn_in: bfloat16 [2304], P('fsdp'), may hold values from -0.5 to 0.5
- gain_ffn_out: bfloat16 [2304], P('fsdp'), may hold values from -0.5 to 0.5
Outputs:
- block_out: bfloat16 [3584, 2304], P(('fsdp', 'ctx'))
- tokens_grad: bfloat16 [3584, 2304], P(('fsdp', 'ctx'))
- query_weight_grad: float32 [2304, 2048], P(('fsdp', 'ctx'), 'tp')
- key_weight_grad: float32 [2304, 1024], P(('fsdp', 'ctx'), 'tp')
- value_weight_grad: float32 [2304, 1024], P(('fsdp', 'ctx'), 'tp')
- output_weight_grad: float32 [2048, 2304], P('tp', ('fsdp', 'ctx'))
- gate_weight_grad: float32 [2304, 9216], P(('fsdp', 'ctx'), 'tp')
- up_weight_grad: float32 [2304, 9216], P(('fsdp', 'ctx'), 'tp')
- down_weight_grad: float32 [9216, 2304], P('tp', ('fsdp', 'ctx'))
- gain_attn_in_grad: float32 [2304], P(('fsdp', 'ctx'))
- gain_attn_out_grad: float32 [2304], P(('fsdp', 'ctx'))
- gain_ffn_in_grad: float32 [2304], P(('fsdp', 'ctx'))
- gain_ffn_out_grad: float32 [2304], P(('fsdp', 'ctx'))
Inputs may be any that keep to these rules, and one draw needn't show every extreme that they name: lengths[g, 0] is the number of live tokens of group g's sequence; in every draw some group has exactly 448 and another exactly 224. Each row of positions is a permutation of 0 to 447.
All inputs are finite; a program needn't handle non-finite values.
Results may differ from a plain program's by a relative error of at most 0.018.
The roundings to bfloat16 on the way count: a program that leaves them out, or rounds other values in their place, can miss the bound.
Values may be sent and summed in bfloat16 or wider, within the bound.
No kernel may reach another device: no remote copies, remote signals or barrier semaphores. Data moves between devices by JAX's collectives and lax.ppermute only.
A program may use at most 640 MiB of HBM per device.

v0:
```python
import functools
import jax
import jax.numpy as jnp
from jax import lax
from jax.sharding import PartitionSpec as P

HEAD_DIM = 256
eps_norm = 1e-06
soft_cap = 50.0
f32 = jnp.float32
b16 = jnp.bfloat16


def rms_scale(field, gain_vec):
    factor = lax.rsqrt(jnp.mean(field * field, axis=-1, keepdims=True) + eps_norm)
    return field * factor * (1.0 + gain_vec)


def gelu_tanh(value_in):
    return (
        0.5
        * value_in
        * (
            1.0
            + jnp.tanh(0.7978845608028654 * (value_in + 0.044715 * value_in * value_in * value_in))
        )
    )


def glu_apply(gate_act, up_act):
    return gelu_tanh(gate_act) * up_act


def norm_back(field, gain_vec, cot_in):
    pullback = jax.vjp(rms_scale, field, gain_vec)[1]
    return pullback(cot_in)


def placement_of(doc_lengths, packed):
    doc_ends = jnp.cumsum(doc_lengths)
    after_end = packed[:, None] >= doc_ends[None, :]
    segment = jnp.sum(after_end.astype(jnp.int32), axis=1)
    inner = packed - jnp.sum(jnp.where(after_end, doc_lengths[None, :], 0), axis=1)
    return (segment, inner)


def angles_of(inner, head_size):
    half_size = head_size // 2
    freq = jnp.power(10000.0, -jnp.arange(half_size, dtype=f32) * (2.0 / head_size))
    return inner.astype(f32)[:, None] * freq[None, :]


def rotate(field, angles):
    half_size = field.shape[-1] // 2
    cosine = jnp.cos(angles)[:, None, :]
    sine = jnp.sin(angles)[:, None, :]
    first_half = field[..., :half_size]
    second_half = field[..., half_size:]
    return jnp.concatenate(
        [first_half * cosine - second_half * sine, second_half * cosine + first_half * sine],
        axis=-1,
    )


def dot(lhs, rhs, dims):
    return lax.dot_general(lhs, rhs, (dims, ((), ())), preferred_element_type=f32)


def swap(piece, axis):
    return lax.ppermute(piece, axis, [(0, 1), (1, 0)])


def hop(piece, step, n):
    return lax.ppermute(piece, "fsdp", [(d, d ^ step) for d in range(n)])


def gather_rows(own, n):
    have = [own]
    bit = n // 2
    while bit:
        have = have + [hop(piece, bit, n) for piece in have]
        bit //= 2
    mine = jnp.concatenate(have)
    return jnp.concatenate([mine, swap(mine, "tp")])


def scatter_rows(part, n):
    rows = part.shape[0] // (2 * n)
    most = n * rows
    both = part[:most] + swap(part[most:].astype(b16), "tp").astype(f32)
    blocks = [both[k * rows : (k + 1) * rows] for k in range(n)]
    bit = 1
    while bit < n:
        keep = len(blocks) // 2
        blocks = [
            blocks[k] + hop(blocks[keep + k].astype(b16), bit, n).astype(f32) for k in range(keep)
        ]
        bit *= 2
    return blocks[0]


def gather_group(own):
    across = swap(own, "ctx")
    beside = swap(jnp.concatenate([own, across]), "tp")
    rows = own.shape[0]
    return jnp.concatenate([own, beside[:rows], across, beside[rows:]])


def scatter_group(part):
    rows = part.shape[0] // 4
    b0, b1, b2, b3 = [part[k * rows : (k + 1) * rows] for k in range(4)]
    got = swap(jnp.concatenate([b1, b3]), "tp")
    return b0 + got[:rows] + swap(b2 + got[rows:], "ctx")


def natural(own, other, index, axis):
    first = jnp.where(index == 0, own, other)
    second = jnp.where(index == 0, other, own)
    return jnp.concatenate([first, second], axis=axis)


def local(
    n,
    tokens,
    cotangent,
    lengths,
    positions,
    query_weight,
    key_weight,
    value_weight,
    output_weight,
    gate_weight,
    up_weight,
    down_weight,
    gain_attn_in,
    gain_attn_out,
    gain_ffn_in,
    gain_ffn_out,
):
    me = lax.axis_index("fsdp")
    ctx = lax.axis_index("ctx")
    tp = lax.axis_index("tp")
    tok_rows, width = tokens.shape
    rows = tok_rows // 2
    head_size = HEAD_DIM
    d_rows = query_weight.shape[0]
    d_half = d_rows // 2
    q_cols = query_weight.shape[1] // 2
    k_cols = key_weight.shape[1] // 2
    q_local = q_cols // head_size
    kv_local = k_cols // head_size
    group_size = q_local // kv_local
    query_scale = head_size ** (-0.5)
    ff_local = gate_weight.shape[1]
    ff_own = ff_local // n
    starts = [c * tok_rows + t * rows for c in (ctx, 1 - ctx) for t in (tp, 1 - tp)]
    packed = jnp.concatenate(
        [lax.dynamic_slice_in_dim(positions[0], start, rows) for start in starts]
    )
    segment, inner = placement_of(lengths[0], packed)
    angles = angles_of(inner, head_size)
    allowed = (segment[:, None] == segment[None, :]) & (inner[None, :] <= inner[:, None])
    mine = lax.dynamic_slice_in_dim(tokens, tp * rows, rows)
    across = swap(mine, "ctx")
    beside = swap(across, "tp")
    seq_group = jnp.concatenate([tokens, across, beside])
    row_ids = jnp.arange(rows, dtype=jnp.int32)
    seq_ids = jnp.concatenate(
        [
            ctx * tok_rows + jnp.arange(tok_rows, dtype=jnp.int32),
            starts[2] + row_ids,
            starts[3] + row_ids,
        ]
    )
    pick = (packed[:, None] == seq_ids[None, :]).astype(b16)
    slot_in = dot(pick, seq_group, ((1,), (0,)))
    resid_in = slot_in[:rows]
    qkv_own = jnp.concatenate(
        [
            lax.dynamic_slice_in_dim(query_weight, ctx * q_cols, q_cols, 1),
            lax.dynamic_slice_in_dim(key_weight, ctx * k_cols, k_cols, 1),
            lax.dynamic_slice_in_dim(value_weight, ctx * k_cols, k_cols, 1),
        ],
        axis=1,
    )
    qkv_weight = lax.all_gather(qkv_own, "fsdp", axis=0, tiled=True)
    out_own = lax.dynamic_slice_in_dim(output_weight, ctx * q_cols, q_cols, 0).T
    out_weight = lax.all_gather(out_own, "fsdp", axis=0, tiled=True)
    gains = lax.all_gather(
        jnp.concatenate([gain_attn_in, gain_attn_out, gain_ffn_in, gain_ffn_out])
        .astype(f32)
        .reshape(1, 4 * d_rows),
        "fsdp",
        axis=0,
        tiled=True,
    )
    gains = gains.reshape(n, 4, d_rows).transpose(1, 0, 2).reshape(4, width)
    ffn_own = jnp.stack([gate_weight, up_weight, down_weight.T])
    ffn_own = ffn_own.reshape(3, 2, d_half, n, ff_own).transpose(3, 1, 0, 2, 4)
    ffn_own = lax.dynamic_index_in_dim(ffn_own, ctx, 1, keepdims=False)
    ffn_full = [jnp.zeros((n, 2, d_half, ff_own), b16) for _ in range(3)]
    for k in range(n):
        piece = lax.dynamic_index_in_dim(ffn_own, me ^ k, 0, keepdims=False)
        if k:
            piece = hop(piece, k, n)
        second = swap(piece, "ctx")
        for which in range(3):
            for half, side in ((piece, ctx), (second, 1 - ctx)):
                ffn_full[which] = lax.dynamic_update_slice(
                    ffn_full[which], half[which][None, None], (me ^ k, side, 0, 0)
                )
    gate_full, up_full, down_full = [full.reshape(width, ff_own) for full in ffn_full]
    normed_attn = rms_scale(slot_in, gains[0]).astype(b16)
    qkv = dot(normed_attn, qkv_weight, ((1,), (0,)))
    all_rows = 2 * tok_rows
    query_lin = qkv[:, :q_cols].reshape(all_rows, q_local, head_size)
    key_lin = qkv[:, q_cols : q_cols + k_cols].reshape(all_rows, kv_local, head_size)
    values = qkv[:, q_cols + k_cols :].astype(b16).reshape(all_rows, kv_local, head_size)
    queries = (rotate(query_lin, angles) * query_scale).astype(b16)
    queries = queries.reshape(all_rows, kv_local, group_size, head_size)
    keys = rotate(key_lin, angles).astype(b16)
    raw_scores = jnp.einsum("qkgd,skd->kgqs", queries, keys, preferred_element_type=f32)
    tanh_ratio = jnp.tanh(raw_scores / soft_cap)
    masked = jnp.where(allowed[None, None], soft_cap * tanh_ratio, -1e30)
    row_peak = jnp.max(masked, axis=-1, keepdims=True)
    exp_terms = jnp.exp(masked - row_peak)
    probs = exp_terms / jnp.sum(exp_terms, axis=-1, keepdims=True)
    probs_low = probs.astype(b16)
    attended = (
        jnp.einsum("kgqs,skd->qkgd", probs_low, values, preferred_element_type=f32)
        .reshape(all_rows, q_cols)
        .astype(b16)
    )
    attn_out = scatter_group(dot(attended, out_weight, ((1,), (1,))))
    middle = resid_in + rms_scale(attn_out, gains[1])
    normed_ffn = gather_rows(rms_scale(middle, gains[2]).astype(b16), n)
    gate_act = dot(normed_ffn, gate_full, ((1,), (0,)))
    up_act = dot(normed_ffn, up_full, ((1,), (0,)))
    hidden = glu_apply(gate_act, up_act).astype(b16)
    ffn_out = scatter_rows(dot(hidden, down_full, ((1,), (1,))), n)
    block_own = (middle + rms_scale(ffn_out, gains[3])).astype(b16)
    block_out = natural(block_own, swap(block_own, "tp"), tp, 0)
    d_out = lax.dynamic_slice_in_dim(cotangent, tp * rows, rows).astype(f32)
    d_ffn_raw, gain_four_term = norm_back(ffn_out, gains[3], d_out)
    d_ffn_out = gather_rows(d_ffn_raw.astype(b16), n)
    d_hidden = dot(d_ffn_out, down_full, ((1,), (0,)))
    d_gate_raw, d_up_raw = jax.vjp(glu_apply, gate_act, up_act)[1](d_hidden)
    d_gate = d_gate_raw.astype(b16)
    d_up = d_up_raw.astype(b16)
    d_normed_ffn = scatter_rows(
        dot(d_gate, gate_full, ((1,), (1,))) + dot(d_up, up_full, ((1,), (1,))), n
    )
    ffn_terms = [
        dot(normed_ffn, d_gate, ((0,), (0,))),
        dot(normed_ffn, d_up, ((0,), (0,))),
        dot(d_ffn_out, hidden, ((0,), (0,))),
    ]
    ffn_terms = [term.reshape(n, 2, d_half, ff_own) for term in ffn_terms]
    ffn_keep = [lax.dynamic_index_in_dim(term, ctx, 1, keepdims=False) for term in ffn_terms]
    ffn_send = [
        lax.dynamic_index_in_dim(term, 1 - ctx, 1, keepdims=False).astype(b16) for term in ffn_terms
    ]
    ffn_sum = [keep + swap(send, "ctx").astype(f32) for keep, send in zip(ffn_keep, ffn_send)]
    ffn_low = jnp.stack([term.astype(b16) for term in ffn_sum], axis=1)
    ffn_grads = ffn_sum
    for k in range(1, n):
        piece = hop(lax.dynamic_index_in_dim(ffn_low, me ^ k, 0, keepdims=False), k, n)
        ffn_grads = [
            lax.dynamic_update_index_in_dim(grad, piece[which].astype(f32), me ^ k, 0)
            for which, grad in enumerate(ffn_grads)
        ]
    gate_weight_grad = ffn_grads[0].transpose(1, 0, 2).reshape(d_half, ff_local)
    up_weight_grad = ffn_grads[1].transpose(1, 0, 2).reshape(d_half, ff_local)
    down_weight_grad = ffn_grads[2].transpose(0, 2, 1).reshape(ff_local, d_half)
    d_middle_part, gain_three_term = norm_back(middle, gains[2], d_normed_ffn)
    d_middle = d_out + d_middle_part
    d_attn_raw, gain_two_term = norm_back(attn_out, gains[1], d_middle)
    d_attn_out = gather_group(d_attn_raw.astype(b16))
    d_attended = dot(d_attn_out, out_weight, ((1,), (0,))).astype(b16)
    d_att = d_attended.reshape(all_rows, kv_local, group_size, head_size)
    d_probs = jnp.einsum("qkgd,skd->kgqs", d_att, values, preferred_element_type=f32)
    d_soft = probs * (d_probs - jnp.sum(probs * d_probs, axis=-1, keepdims=True))
    d_scores = (d_soft * (1.0 - tanh_ratio * tanh_ratio)).astype(b16)
    d_queries = jnp.einsum("kgqs,skd->qkgd", d_scores, keys, preferred_element_type=f32)
    d_keys = jnp.einsum("kgqs,qkgd->skd", d_scores, queries, preferred_element_type=f32)
    d_values = jnp.einsum("kgqs,qkgd->skd", probs_low, d_att, preferred_element_type=f32)
    d_query_lin = (
        rotate(d_queries.reshape(all_rows, q_local, head_size) * query_scale, -angles)
        .reshape(all_rows, q_cols)
        .astype(b16)
    )
    d_key_lin = rotate(d_keys, -angles).reshape(all_rows, k_cols).astype(b16)
    d_value = d_values.reshape(all_rows, k_cols).astype(b16)
    d_qkv = jnp.concatenate([d_query_lin, d_key_lin, d_value], axis=1)
    d_normed_attn = scatter_group(dot(d_qkv, qkv_weight, ((1,), (1,))))
    resid_part, gain_one_term = norm_back(resid_in, gains[0], d_normed_attn)
    slot_grad = gather_group((d_middle + resid_part).astype(b16))
    place = (
        (ctx * tok_rows + jnp.arange(tok_rows, dtype=jnp.int32))[:, None] == packed[None, :]
    ).astype(b16)
    tokens_grad = dot(place, slot_grad, ((1,), (0,))).astype(b16)
    attn_terms = jnp.concatenate(
        [dot(normed_attn, d_qkv, ((0,), (0,))), dot(d_attn_out, attended, ((0,), (0,)))], axis=1
    ).astype(b16)
    attn_rows = lax.psum_scatter(attn_terms, "fsdp", scatter_dimension=0, tiled=True)
    attn_rows = attn_rows.reshape(2, d_half, -1)
    attn_own = lax.dynamic_index_in_dim(attn_rows, ctx, 0, keepdims=False)
    attn_other = swap(lax.dynamic_index_in_dim(attn_rows, 1 - ctx, 0, keepdims=False), "ctx")
    edges = [0, q_cols, q_cols + k_cols, q_cols + 2 * k_cols, 2 * q_cols + 2 * k_cols]
    attn_grads = [
        natural(attn_own[:, a:b].astype(f32), attn_other[:, a:b].astype(f32), ctx, 1)
        for a, b in zip(edges[:-1], edges[1:])
    ]
    gain_terms = jnp.stack([gain_one_term, gain_two_term, gain_three_term, gain_four_term])
    gain_terms = gain_terms.reshape(4, 2 * n, d_half).transpose(1, 0, 2).reshape(2 * n, 4 * d_half)
    gain_terms = gain_terms + swap(gain_terms, "tp")
    gain_rows = lax.psum_scatter(gain_terms, ("fsdp", "ctx"), scatter_dimension=0, tiled=True)
    gain_rows = gain_rows.reshape(4, d_half)
    return (
        block_out,
        tokens_grad,
        attn_grads[0],
        attn_grads[1],
        attn_grads[2],
        attn_grads[3].T,
        gate_weight_grad,
        up_weight_grad,
        down_weight_grad,
        gain_rows[0],
        gain_rows[1],
        gain_rows[2],
        gain_rows[3],
    )


def solution(mesh):
    in_specs = (
        P(("fsdp", "ctx"), None),
        P(("fsdp", "ctx"), None),
        P("fsdp", None),
        P("fsdp", None),
        P("fsdp", "tp"),
        P("fsdp", "tp"),
        P("fsdp", "tp"),
        P("tp", "fsdp"),
        P("fsdp", "tp"),
        P("fsdp", "tp"),
        P("tp", "fsdp"),
        P("fsdp"),
        P("fsdp"),
        P("fsdp"),
        P("fsdp"),
    )
    out_specs = (
        P(("fsdp", "ctx"), None),
        P(("fsdp", "ctx"), None),
        P(("fsdp", "ctx"), "tp"),
        P(("fsdp", "ctx"), "tp"),
        P(("fsdp", "ctx"), "tp"),
        P("tp", ("fsdp", "ctx")),
        P(("fsdp", "ctx"), "tp"),
        P(("fsdp", "ctx"), "tp"),
        P("tp", ("fsdp", "ctx")),
        P(("fsdp", "ctx")),
        P(("fsdp", "ctx")),
        P(("fsdp", "ctx")),
        P(("fsdp", "ctx")),
    )
    step = functools.partial(local, mesh.shape["fsdp"])
    return jax.shard_map(step, mesh=mesh, in_specs=in_specs, out_specs=out_specs, check_vma=False)
```

profile of v0, /device:TPU:0, one launch (start us, length us, event | category | flops | bytes accessed | tf_op | source)
XLA Modules:
  0.0 1150.1 jit_solution(1037541501683271396)
XLA Ops:
  15.2 31.4 %all-gather = f32[8,1,1152]{2,1,0:T(1,128)S(1)} all-gather(f32[1,1,1152]{2,1,0:T(1,128)S(1)} %bitcast_convert_fusion.2), channel_id=1, replica_groups=mesh['fsdp'=8,'ctx'=2,'tp'=2] {'fsdp'}, dimensions={0}, use_global_device_ids=true | all-gather | bytes 41472 | tf_op jit(solution)/shard_map/all_gather | solution.py:189
  53.8 40.0 %all-gather.4.cloned.1.call-done = bf16[2304,1024]{1,0:T(8,128)(2,1)} async-done(((bf16[288,1024]{1,0:T(8,128)(2,1)}), bf16[2304,1024]{1,0:T(8,128)(2,1)}) %all-gather.4.cloned.1.call-update) | async-done | bytes 4718608 | tf_op jit(solution)/shard_map/all_gather | solution.py:186
  108.9 37.8 %all-gather.6.cloned.1.call-done = bf16[2304,512]{1,0:T(8,128)(2,1)} async-done(((bf16[288,512]{1,0:T(8,128)(2,1)}), bf16[2304,512]{1,0:T(8,128)(2,1)}) %all-gather.6.cloned.1.call-update) | async-done | bytes 2359312 | tf_op jit(solution)/shard_map/all_gather | solution.py:188
  211.9 22.0 %collective-permute-done.5 = bf16[112,2304]{1,0:T(8,128)(2,1)S(1)} collective-permute-done((bf16[112,2304]{1,0:T(8,128)(2,1)S(1)}, bf16[112,2304]{1,0:T(8,128)(2,1)S(1)}, u32[]{:S(2)}, u32[]{:S(2)}) %collective-permute-start.5) | collective-permute-done | bytes 516128 | tf_op jit(solution)/shard_map/ppermute | solution.py:74
  248.9 10.6 collective-permute-done.8
  271.4 21.1 %collective-permute-done.10 = bf16[112,2304]{1,0:T(8,128)(2,1)S(1)} collective-permute-done((bf16[112,2304]{1,0:T(8,128)(2,1)S(1)}, bf16[112,2304]{1,0:T(8,128)(2,1)S(1)}, u32[]{:S(2)}, u32[]{:S(2)}) %collective-permute-start.10) | collective-permute-done | bytes 516128 | tf_op jit(solution)/shard_map/ppermute | solution.py:74
  323.5 38.0 %collective-permute-done.19 = bf16[3,144,576]{2,1,0:T(8,128)(2,1)S(1)} collective-permute-done((bf16[3,144,576]{2,1,0:T(8,128)(2,1)}, bf16[3,144,576]{2,1,0:T(8,128)(2,1)S(1)}, u32[]{:S(2)}, u32[]{:S(2)}) %collective-permute-start.19) | collective-permute-done | bytes 497696 | tf_op jit(solution)/shard_map/ppermute | solution.py:74
  366.8 18.4 %collective-permute-done.21 = bf16[3,144,576]{2,1,0:T(8,128)(2,1)S(1)} collective-permute-done((bf16[3,144,576]{2,1,0:T(8,128)(2,1)}, bf16[3,144,576]{2,1,0:T(8,128)(2,1)S(1)}, u32[]{:S(2)}, u32[]{:S(2)}) %collective-permute-start.21) | collective-permute-done | bytes 497696 | tf_op jit(solution)/shard_map/ppermute | solution.py:74
  402.2 10.2 collective-permute-done.22
  438.4 11.5 %fusion.192 = f32[1792,576]{0,1:T(8,128)} fusion(bf16[1792,2304]{1,0:T(8,128)(2,1)S(1)} %constant_dynamic-update-slice_fusion.8, bf16[2304,576]{1,0:T(8,128)(2,1)} %bitcast.35), kind=kOutput, calls=%fused_computation.456 | convolution fusion | flops 4756340736 | bytes 15040512 | tf_op jit(solution)/shard_map/dot_general | solution.py:66
  449.9 14.4 %multiply_convert_fusion.1 = (bf16[1792,576]{0,1:T(8,128)(2,1)}, f32[1792,576]{0,1:T(8,128)}) fusion(f32[1792,576]{0,1:T(8,128)} %fusion.192, bf16[1792,2304]{1,0:T(8,128)(2,1)} %copy-done.57, bf16[2304,576]{1,0:T(8,128)(2,1)} %bitcast.52), kind=kOutput, calls=%fused_computation.20 | convolution fusion | flops 4766662656 | bytes 21233664 | tf_op jit(solution)/shard_map/dot_general | solution.py:66
  488.3 10.3 fusion.180
  504.5 11.1 collective-permute-done.32
  526.7 11.1 collective-permute-done.31
  548.1 15.2 %collective-permute-done.30 = bf16[112,2304]{1,0:T(8,128)(2,1)S(1)} collective-permute-done((bf16[112,2304]{1,0:T(8,128)(2,1)}, bf16[112,2304]{1,0:T(8,128)(2,1)S(1)}, u32[]{:S(2)}, u32[]{:S(2)}) %collective-permute-start.30) | collective-permute-done | bytes 516128 | tf_op jit(solution)/shard_map/ppermute | solution.py:74
  573.5 18.7 %collective-permute-done.36 = bf16[112,2304]{1,0:T(8,128)(2,1)S(1)} collective-permute-done((bf16[112,2304]{1,0:T(8,128)(2,1)S(1)}, bf16[112,2304]{1,0:T(8,128)(2,1)S(1)}, u32[]{:S(2)}, u32[]{:S(2)}) %collective-permute-start.36) | collective-permute-done | bytes 516128 | tf_op jit(solution)/shard_map/ppermute | solution.py:74
  594.4 11.5 collective-permute-done.38
  607.6 10.3 collective-permute-done.41
  641.3 12.4 %fusion.3 = (bf16[1792,576]{0,1:T(8,128)(2,1)S(1)}, bf16[1792,576]{0,1:T(8,128)(2,1)S(1)}) fusion(f32[1792,576]{0,1:T(8,128)S(1)} %copy-done.81, f32[1792,576]{0,1:T(8,128)} %get-tuple-element.226, bf16[1792,2304]{1,0:T(8,128)(2,1)} %copy-done.55, bf16[2304,576]{1,0:T(8,128)(2,1)S(1)} %bitcast.455), kind=kOutput, calls=%fused_computation.16 | convolution fusion | flops 4785242112 | bytes 23298048 | tf_op jit(solution)/shard_map/dot_general | solution.py:66
  653.7 13.6 %fusion.194 = f32[1792,2304]{1,0:T(8,128)} fusion(bf16[1792,576]{0,1:T(8,128)(2,1)S(1)} %get-tuple-element.63, bf16[2304,576]{1,0:T(8,128)(2,1)} %bitcast.52), kind=kOutput, calls=%fused_computation.458 | convolution fusion | flops 4756340736 | bytes 21233664 | tf_op jit(solution)/shard_map/dot_general | solution.py:66
  667.3 15.2 %convolution_add_fusion = f32[1792,2304]{1,0:T(8,128)} fusion(f32[1792,2304]{1,0:T(8,128)} %fusion.194, bf16[1792,576]{0,1:T(8,128)(2,1)S(1)} %get-tuple-element.62, bf16[2304,576]{1,0:T(8,128)(2,1)} %bitcast.35), kind=kOutput, calls=%fused_computation | convolution fusion | flops 4760469504 | bytes 37748736 | tf_op jit(solution)/shard_map/dot_general | solution.py:66
  693.5 10.3 fusion.177
  709.0 11.1 collective-permute-done.49
  731.2 11.1 collective-permute-done.48
  752.5 14.1 %collective-permute-done.47 = bf16[112,2304]{1,0:T(8,128)(2,1)S(1)} collective-permute-done((bf16[112,2304]{1,0:T(8,128)(2,1)S(1)}, bf16[112,2304]{1,0:T(8,128)(2,1)S(1)}, u32[]{:S(2)}, u32[]{:S(2)}) %collective-permute-start.47) | collective-permute-done | bytes 516128 | tf_op jit(solution)/shard_map/ppermute | solution.py:74
  804.8 10.3 copy.101
  865.8 28.8 %collective-permute-done.60 = bf16[8,144,576]{2,1,0:T(8,128)(2,1)} collective-permute-done((bf16[8,144,576]{2,1,0:T(8,128)(2,1)}, bf16[8,144,576]{2,1,0:T(8,128)(2,1)}, u32[]{:S(2)}, u32[]{:S(2)}) %collective-permute-start.60) | collective-permute-done | bytes 1327136 | tf_op jit(solution)/shard_map/ppermute | solution.py:70
  897.2 28.2 %collective-permute-done.61 = bf16[8,144,576]{2,1,0:T(8,128)(2,1)} collective-permute-done((bf16[8,144,576]{2,1,0:T(8,128)(2,1)}, bf16[8,144,576]{2,1,0:T(8,128)(2,1)}, u32[]{:S(2)}, u32[]{:S(2)}) %collective-permute-start.61) | collective-permute-done | bytes 1327136 | tf_op jit(solution)/shard_map/ppermute | solution.py:70
  959.9 16.9 %collective-permute-done.63 = bf16[3,144,576]{2,1,0:T(8,128)(2,1)S(1)} collective-permute-done((bf16[3,144,576]{2,1,0:T(8,128)(2,1)S(1)}, bf16[3,144,576]{2,1,0:T(8,128)(2,1)S(1)}, u32[]{:S(2)}, u32[]{:S(2)}) %collective-permute-start.63) | collective-permute-done | bytes 497696 | tf_op jit(solution)/shard_map/ppermute | solution.py:74
  978.4 11.1 collective-permute-done.64
  992.9 10.2 collective-permute-done.67
  1038.3 90.6 %all-reduce = f32[16,576]{1,0:T(8,128)S(1)} all-reduce(f32[16,576]{1,0:T(8,128)S(1)} %add.561), channel_id=3, replica_groups=mesh['fsdp'=8,'ctx'=2,'tp'=2] {'fsdp','ctx'}, use_global_device_ids=true, to_apply=%region_17.18.clone | all-reduce | flops 9216 | bytes 73728
  (503 shorter events, 506.4 us)
Async XLA Ops:
  7.3 86.5 %all-gather.4.cloned.1.call-start = ((), (), s32[]{:S(2)}) async-start(), calls=%async_computation.1 | async-start | bytes 5308416 | tf_op jit(solution)/shard_map/all_gather | solution.py:186
  10.2 136.4 %all-gather.6.cloned.1.call-start = ((), (), s32[]{:S(2)}) async-start(), calls=%async_computation.2 | async-start | bytes 2654208 | tf_op jit(solution)/shard_map/all_gather | solution.py:188
  10.3 37.3 %collective-permute-start = (bf16[112,2304]{1,0:T(8,128)(2,1)S(1)}, bf16[112,2304]{1,0:T(8,128)(2,1)S(1)}, u32[]{:S(2)}, u32[]{:S(2)}) collective-permute-start(bf16[112,2304]{1,0:T(8,128)(2,1)S(1)} %constant_dynamic-slice_fusion.11), channel_id=1, source_target_pairs={{0,2},{2,0},{1,3},{3,1},{4,6},{6,4},{5,7},{7,5},{8,10},{10,8},{9,1... | collective-permute-start | bytes 1548296 | tf_op jit(solution)/shard_map/ppermute | solution.py:70
  14.1 1116.0 %reduce-scatter.4.cloned.1.call-start = ((), (), s32[]{:S(2)}) async-start(), calls=%async_computation.3 | async-start | bytes 7962624 | tf_op jit(solution)/shard_map/reduce_scatter | solution.py:305
  198.0 114.1 %collective-permute-start.12 = (bf16[3,144,576]{2,1,0:T(8,128)(2,1)S(1)}, bf16[3,144,576]{2,1,0:T(8,128)(2,1)}, u32[]{:S(2)}, u32[]{:S(2)}) collective-permute-start(bf16[3,144,576]{2,1,0:T(8,128)(2,1)S(1)} %bitcast.457), channel_id=1, source_target_pairs={{0,2},{2,0},{1,3},{3,1},{4,6},{6,4},{5,7},{7,5},{8,10},{10,8},{9,1... | collective-permute-start | bytes 1493000 | tf_op jit(solution)/shard_map/ppermute | solution.py:70
  199.6 100.0 %collective-permute-start.13 = (bf16[3,144,576]{2,1,0:T(8,128)(2,1)S(1)}, bf16[3,144,576]{2,1,0:T(8,128)(2,1)}, u32[]{:S(2)}, u32[]{:S(2)}) collective-permute-start(bf16[3,144,576]{2,1,0:T(8,128)(2,1)S(1)} %bitcast.466), channel_id=1, source_target_pairs={{0,4},{4,0},{8,12},{12,8},{16,20},{20,16},{24,28},{28,24},{1,5},{5... | collective-permute-start | bytes 1493000 | tf_op jit(solution)/shard_map/ppermute | solution.py:74
  201.1 111.1 %collective-permute-start.15 = (bf16[3,144,576]{2,1,0:T(8,128)(2,1)}, bf16[3,144,576]{2,1,0:T(8,128)(2,1)}, u32[]{:S(2)}, u32[]{:S(2)}) collective-permute-start(bf16[3,144,576]{2,1,0:T(8,128)(2,1)} %bitcast.438), channel_id=1, source_target_pairs={{0,8},{4,12},{8,0},{12,4},{16,24},{20,28},{24,16},{28,20},{1,9},{5... | collective-permute-start | bytes 1493000 | tf_op jit(solution)/shard_map/ppermute | solution.py:74
  201.7 32.1 %collective-permute-start.5 = (bf16[112,2304]{1,0:T(8,128)(2,1)S(1)}, bf16[112,2304]{1,0:T(8,128)(2,1)S(1)}, u32[]{:S(2)}, u32[]{:S(2)}) collective-permute-start(bf16[112,2304]{1,0:T(8,128)(2,1)S(1)} %get-tuple-element.43), channel_id=1, source_target_pairs={{0,8},{4,12},{8,0},{12,4},{16,24},{20,28},{24,16},{28,20},{1,9},{5... | collective-permute-start | bytes 1548296 | tf_op jit(solution)/shard_map/ppermute | solution.py:74
  211.0 33.9 %collective-permute-start.6 = (bf16[112,2304]{1,0:T(8,128)(2,1)S(1)}, bf16[112,2304]{1,0:T(8,128)(2,1)S(1)}, u32[]{:S(2)}, u32[]{:S(2)}) collective-permute-start(bf16[112,2304]{1,0:T(8,128)(2,1)S(1)} %collective-permute-done.4), channel_id=1, source_target_pairs={{0,8},{4,12},{8,0},{12,4},{16,24},{20,28},{24,16},{28,20},{1,9},{5... | collective-permute-start | bytes 1548296 | tf_op jit(solution)/shard_map/ppermute | solution.py:74
  259.4 33.0 %collective-permute-start.10 = (bf16[112,2304]{1,0:T(8,128)(2,1)S(1)}, bf16[112,2304]{1,0:T(8,128)(2,1)S(1)}, u32[]{:S(2)}, u32[]{:S(2)}) collective-permute-start(bf16[112,2304]{1,0:T(8,128)(2,1)S(1)} %collective-permute-done.6), channel_id=1, source_target_pairs={{0,4},{4,0},{8,12},{12,8},{16,20},{20,16},{24,28},{28,24},{1,5},{5... | collective-permute-start | bytes 1548296 | tf_op jit(solution)/shard_map/ppermute | solution.py:74
  270.5 51.1 %collective-permute-start.17 = (bf16[3,144,576]{2,1,0:T(8,128)(2,1)S(1)}, bf16[3,144,576]{2,1,0:T(8,128)(2,1)}, u32[]{:S(2)}, u32[]{:S(2)}) collective-permute-start(bf16[3,144,576]{2,1,0:T(8,128)(2,1)S(1)} %bitcast.465), channel_id=1, source_target_pairs={{0,12},{4,8},{8,4},{12,0},{16,28},{20,24},{24,20},{28,16},{1,13},{... | collective-permute-start | bytes 1493000 | tf_op jit(solution)/shard_map/ppermute | solution.py:74
  293.3 142.6 %collective-permute-start.11 = (bf16[896,2304]{1,0:T(8,128)(2,1)}, bf16[896,2304]{1,0:T(8,128)(2,1)}, u32[]{:S(2)}, u32[]{:S(2)}) collective-permute-start(bf16[896,2304]{1,0:T(8,128)(2,1)} %get-tuple-element.191), channel_id=1, source_target_pairs={{0,1},{1,0},{2,3},{3,2},{4,5},{5,4},{6,7},{7,6},{8,9},{9,8},{10,11... | collective-permute-start | bytes 12386312 | tf_op jit(solution)/shard_map/ppermute | solution.py:70
  312.1 49.4 %collective-permute-start.19 = (bf16[3,144,576]{2,1,0:T(8,128)(2,1)}, bf16[3,144,576]{2,1,0:T(8,128)(2,1)S(1)}, u32[]{:S(2)}, u32[]{:S(2)}) collective-permute-start(bf16[3,144,576]{2,1,0:T(8,128)(2,1)} %bitcast.470), channel_id=1, source_target_pairs={{0,16},{4,20},{8,24},{12,28},{16,0},{20,4},{24,8},{28,12},{1,17},{... | collective-permute-start | bytes 1493000 | tf_op jit(solution)/shard_map/ppermute | solution.py:74
  312.2 51.3 %collective-permute-start.16 = (bf16[3,144,576]{2,1,0:T(8,128)(2,1)}, bf16[3,144,576]{2,1,0:T(8,128)(2,1)S(1)}, u32[]{:S(2)}, u32[]{:S(2)}) collective-permute-start(bf16[3,144,576]{2,1,0:T(8,128)(2,1)} %collective-permute-done.15), channel_id=1, source_target_pairs={{0,2},{2,0},{1,3},{3,1},{4,6},{6,4},{5,7},{7,5},{8,10},{10,8},{9,1... | collective-permute-start | bytes 1493000 | tf_op jit(solution)/shard_map/ppermute | solution.py:70
  316.9 68.3 %collective-permute-start.21 = (bf16[3,144,576]{2,1,0:T(8,128)(2,1)}, bf16[3,144,576]{2,1,0:T(8,128)(2,1)S(1)}, u32[]{:S(2)}, u32[]{:S(2)}) collective-permute-start(bf16[3,144,576]{2,1,0:T(8,128)(2,1)} %bitcast.469), channel_id=1, source_target_pairs={{0,20},{4,16},{8,28},{12,24},{16,4},{20,0},{24,12},{28,8},{1,21},{... | collective-permute-start | bytes 1493000 | tf_op jit(solution)/shard_map/ppermute | solution.py:74
  321.6 66.0 %collective-permute-start.23 = (bf16[3,144,576]{2,1,0:T(8,128)(2,1)S(1)}, bf16[3,144,576]{2,1,0:T(8,128)(2,1)S(1)}, u32[]{:S(2)}, u32[]{:S(2)}) collective-permute-start(bf16[3,144,576]{2,1,0:T(8,128)(2,1)S(1)} %bitcast.468), channel_id=1, source_target_pairs={{0,24},{4,28},{8,16},{12,20},{16,8},{20,12},{24,0},{28,4},{1,25},{... | collective-permute-start | bytes 1493000 | tf_op jit(solution)/shard_map/ppermute | solution.py:74
  389.1 35.2 %collective-permute-start.24 = (bf16[3,144,576]{2,1,0:T(8,128)(2,1)S(1)}, bf16[3,144,576]{2,1,0:T(8,128)(2,1)S(1)}, u32[]{:S(2)}, u32[]{:S(2)}) collective-permute-start(bf16[3,144,576]{2,1,0:T(8,128)(2,1)S(1)} %collective-permute-done.23), channel_id=1, source_target_pairs={{0,2},{2,0},{1,3},{3,1},{4,6},{6,4},{5,7},{7,5},{8,10},{10,8},{9,1... | collective-permute-start | bytes 1493000 | tf_op jit(solution)/shard_map/ppermute | solution.py:70
  389.7 45.4 %collective-permute-start.26 = (bf16[3,144,576]{2,1,0:T(8,128)(2,1)S(1)}, bf16[3,144,576]{2,1,0:T(8,128)(2,1)S(1)}, u32[]{:S(2)}, u32[]{:S(2)}) collective-permute-start(bf16[3,144,576]{2,1,0:T(8,128)(2,1)S(1)} %collective-permute-done.25), channel_id=1, source_target_pairs={{0,2},{2,0},{1,3},{3,1},{4,6},{6,4},{5,7},{7,5},{8,10},{10,8},{9,1... | collective-permute-start | bytes 1493000 | tf_op jit(solution)/shard_map/ppermute | solution.py:70
  503.1 34.7 %collective-permute-start.31 = (bf16[112,2304]{1,0:T(8,128)(2,1)S(1)}, bf16[112,2304]{1,0:T(8,128)(2,1)S(1)}, u32[]{:S(2)}, u32[]{:S(2)}) collective-permute-start(bf16[112,2304]{1,0:T(8,128)(2,1)S(1)} %get-tuple-element.82), channel_id=1, source_target_pairs={{0,4},{4,0},{8,12},{12,8},{16,20},{20,16},{24,28},{28,24},{1,5},{5... | collective-permute-start | bytes 1548296 | tf_op jit(solution)/shard_map/ppermute | solution.py:74
  572.0 35.4 %collective-permute-start.39 = (bf16[112,2304]{1,0:T(8,128)(2,1)S(1)}, bf16[112,2304]{1,0:T(8,128)(2,1)S(1)}, u32[]{:S(2)}, u32[]{:S(2)}) collective-permute-start(bf16[112,2304]{1,0:T(8,128)(2,1)S(1)} %get-tuple-element.37), channel_id=1, source_target_pairs={{0,4},{4,0},{8,12},{12,8},{16,20},{20,16},{24,28},{28,24},{1,5},{5... | collective-permute-start | bytes 1548296 | tf_op jit(solution)/shard_map/ppermute | solution.py:74
  707.5 34.7 %collective-permute-start.48 = (bf16[112,2304]{1,0:T(8,128)(2,1)S(1)}, bf16[112,2304]{1,0:T(8,128)(2,1)S(1)}, u32[]{:S(2)}, u32[]{:S(2)}) collective-permute-start(bf16[112,2304]{1,0:T(8,128)(2,1)S(1)} %get-tuple-element.78), channel_id=1, source_target_pairs={{0,4},{4,0},{8,12},{12,8},{16,20},{20,16},{24,28},{28,24},{1,5},{5... | collective-permute-start | bytes 1548296 | tf_op jit(solution)/shard_map/ppermute | solution.py:74
  827.7 35.2 %collective-permute-start.59 = (bf16[8,144,576]{2,1,0:T(8,128)(2,1)S(1)}, bf16[8,144,576]{2,1,0:T(8,128)(2,1)}, u32[]{:S(2)}, u32[]{:S(2)}) collective-permute-start(bf16[8,144,576]{2,1,0:T(8,128)(2,1)S(1)} %fusion.24), channel_id=1, source_target_pairs={{0,2},{2,0},{1,3},{3,1},{4,6},{6,4},{5,7},{7,5},{8,10},{10,8},{9,1... | collective-permute-start | bytes 3981320 | tf_op jit(solution)/shard_map/ppermute | solution.py:70
  841.1 53.4 %collective-permute-start.60 = (bf16[8,144,576]{2,1,0:T(8,128)(2,1)}, bf16[8,144,576]{2,1,0:T(8,128)(2,1)}, u32[]{:S(2)}, u32[]{:S(2)}) collective-permute-start(bf16[8,144,576]{2,1,0:T(8,128)(2,1)} %fusion.25), channel_id=1, source_target_pairs={{0,2},{2,0},{1,3},{3,1},{4,6},{6,4},{5,7},{7,5},{8,10},{10,8},{9,1... | collective-permute-start | bytes 3981320 | tf_op jit(solution)/shard_map/ppermute | solution.py:70
  852.2 73.1 %collective-permute-start.61 = (bf16[8,144,576]{2,1,0:T(8,128)(2,1)}, bf16[8,144,576]{2,1,0:T(8,128)(2,1)}, u32[]{:S(2)}, u32[]{:S(2)}) collective-permute-start(bf16[8,144,576]{2,1,0:T(8,128)(2,1)} %fusion.26), channel_id=1, source_target_pairs={{0,2},{2,0},{1,3},{3,1},{4,6},{6,4},{5,7},{7,5},{8,10},{10,8},{9,1... | collective-permute-start | bytes 3981320 | tf_op jit(solution)/shard_map/ppermute | solution.py:70
  858.0 72.8 %collective-permute-start.54 = (f32[224,2304]{1,0:T(8,128)}, f32[224,2304]{1,0:T(8,128)}, u32[]{:S(2)}, u32[]{:S(2)}) collective-permute-start(f32[224,2304]{1,0:T(8,128)} %pad_maximum_fusion.4), channel_id=1, source_target_pairs={{0,1},{1,0},{2,3},{3,2},{4,5},{5,4},{6,7},{7,6},{8,9},{9,8},{10,11... | collective-permute-start | bytes 6193160 | tf_op jit(solution)/shard_map/ppermute | solution.py:70
  858.7 74.2 %collective-permute-start.35 = (bf16[112,2304]{1,0:T(8,128)(2,1)}, bf16[112,2304]{1,0:T(8,128)(2,1)S(1)}, u32[]{:S(2)}, u32[]{:S(2)}) collective-permute-start(bf16[112,2304]{1,0:T(8,128)(2,1)} %get-tuple-element.92), channel_id=1, source_target_pairs={{0,1},{1,0},{2,3},{3,2},{4,5},{5,4},{6,7},{7,6},{8,9},{9,8},{10,11... | collective-permute-start | bytes 1548296 | tf_op jit(solution)/shard_map/ppermute | solution.py:70
  935.5 41.3 %collective-permute-start.63 = (bf16[3,144,576]{2,1,0:T(8,128)(2,1)S(1)}, bf16[3,144,576]{2,1,0:T(8,128)(2,1)S(1)}, u32[]{:S(2)}, u32[]{:S(2)}) collective-permute-start(bf16[3,144,576]{2,1,0:T(8,128)(2,1)S(1)} %get-tuple-element.71), channel_id=1, source_target_pairs={{0,8},{4,12},{8,0},{12,4},{16,24},{20,28},{24,16},{28,20},{1,9},{5... | collective-permute-start | bytes 1493000 | tf_op jit(solution)/shard_map/ppermute | solution.py:74
  937.4 52.0 %collective-permute-start.64 = (bf16[3,144,576]{2,1,0:T(8,128)(2,1)S(1)}, bf16[3,144,576]{2,1,0:T(8,128)(2,1)S(1)}, u32[]{:S(2)}, u32[]{:S(2)}) collective-permute-start(bf16[3,144,576]{2,1,0:T(8,128)(2,1)S(1)} %get-tuple-element.70), channel_id=1, source_target_pairs={{0,12},{4,8},{8,4},{12,0},{16,28},{20,24},{24,20},{28,16},{1,13},{... | collective-permute-start | bytes 1493000 | tf_op jit(solution)/shard_map/ppermute | solution.py:74
  938.1 53.5 %collective-permute-start.65 = (bf16[3,144,576]{2,1,0:T(8,128)(2,1)S(1)}, bf16[3,144,576]{2,1,0:T(8,128)(2,1)S(1)}, u32[]{:S(2)}, u32[]{:S(2)}) collective-permute-start(bf16[3,144,576]{2,1,0:T(8,128)(2,1)S(1)} %get-tuple-element.69), channel_id=1, source_target_pairs={{0,16},{4,20},{8,24},{12,28},{16,0},{20,4},{24,8},{28,12},{1,17},{... | collective-permute-start | bytes 1493000 | tf_op jit(solution)/shard_map/ppermute | solution.py:74
  943.3 49.5 %collective-permute-start.66 = (bf16[3,144,576]{2,1,0:T(8,128)(2,1)S(1)}, bf16[3,144,576]{2,1,0:T(8,128)(2,1)S(1)}, u32[]{:S(2)}, u32[]{:S(2)}) collective-permute-start(bf16[3,144,576]{2,1,0:T(8,128)(2,1)S(1)} %get-tuple-element.68), channel_id=1, source_target_pairs={{0,20},{4,16},{8,28},{12,24},{16,4},{20,0},{24,12},{28,8},{1,21},{... | collective-permute-start | bytes 1493000 | tf_op jit(solution)/shard_map/ppermute | solution.py:74
  956.1 47.1 %collective-permute-start.67 = (bf16[3,144,576]{2,1,0:T(8,128)(2,1)S(1)}, bf16[3,144,576]{2,1,0:T(8,128)(2,1)S(1)}, u32[]{:S(2)}, u32[]{:S(2)}) collective-permute-start(bf16[3,144,576]{2,1,0:T(8,128)(2,1)S(1)} %get-tuple-element.67), channel_id=1, source_target_pairs={{0,24},{4,28},{8,16},{12,20},{16,8},{20,12},{24,0},{28,4},{1,25},{... | collective-permute-start | bytes 1493000 | tf_op jit(solution)/shard_map/ppermute | solution.py:74
  992.8 138.5 %collective-permute-start.57 = (bf16[224,2304]{1,0:T(8,128)(2,1)}, bf16[224,2304]{1,0:T(8,128)(2,1)}, u32[]{:S(2)}, u32[]{:S(2)}) collective-permute-start(bf16[224,2304]{1,0:T(8,128)(2,1)} %pad_maximum_fusion.7), channel_id=1, source_target_pairs={{0,1},{1,0},{2,3},{3,2},{4,5},{5,4},{6,7},{7,6},{8,9},{9,8},{10,11... | collective-permute-start | bytes 3096584 | tf_op jit(solution)/shard_map/ppermute | solution.py:70
  (131 other events, 2197.7 us)
Sparse Core Ops, SparseCore 0:
  10.9 82.8 all-gather.3
  96.5 50.0 all-gather.5
  815.2 151.4 reduce-scatter.3
where the time goes:
time: 1160 us; the launch traced here: 1150 us
  waiting for transfers between devices  571 us (49%)
  local copies, waits for them, and re-layouts  158 us (14%)
  matrix products  132 us (11%)
  blocking collectives  122 us (11%)
  other arithmetic  80.2 us (7%)
  starting transfers between devices  71.3 us (6%)
  between operations  16.4 us (1%)
    ppermute x42, waiting for transfers between devices, hop(): return lax.ppermute(piece, 'fsdp', [(d, d ^ step) for d in range(n)])  338 us
    ppermute x28, waiting for transfers between devices, swap(): return lax.ppermute(piece, axis, [(0, 1), (1, 0)])  155 us
    dot_general x17, matrix products, dot(): lax.dot_general(lhs, rhs, (dims, ((), ())), preferred_element_type=f32)  125 us
    unnamed x1, blocking collectives  90.6 us
    unnamed x207, local copies, waits for them, and re-layouts  58.9 us
    ppermute x42, starting transfers between devices, hop(): return lax.ppermute(piece, 'fsdp', [(d, d ^ step) for d in range(n)])  51.9 us
    all_gather x1, waiting for transfers between devices, local(): qkv_weight = lax.all_gather(qkv_own, 'fsdp', axis=0, tiled=True)  40 us
    all_gather x1, waiting for transfers between devices, local(): out_weight = lax.all_gather(out_own, 'fsdp', axis=0, tiled=True)  37.8 us
  transfers between devices with their start and end apart: 73, of which 48 were waited for; matrix products, arithmetic and copies ran while one was open for 16% of the time, Pallas kernels for 0%

commit v1 on v0

--- a/solution.py
+++ b/solution.py
@@ -137,6 +137,23 @@
     gain_ffn_in,
     gain_ffn_out,
 ):
+
+    def expand_the_circles(field_in, along_dim=0):
+        peer_axis = "fsdp"
+        many = lax.axis_size(peer_axis)
+        row_list = tuple(((dev_i, (dev_i + 1) % many) for dev_i in range(many)))
+
+        def turns_detail(carry_in):
+            if len(carry_in) == many:
+                return carry_in
+            latest = lax.ppermute(carry_in[0], axis_name=peer_axis, perm=row_list)
+            return turns_detail([latest, *carry_in])
+
+        oldest = turns_detail([field_in])
+        response = jnp.concatenate(oldest, axis=along_dim)
+        state_next = lax.axis_index(peer_axis)
+        return jnp.roll(response, (state_next + 1) * field_in.shape[along_dim], axis=along_dim)
+
     me = lax.axis_index("fsdp")
     ctx = lax.axis_index("ctx")
     tp = lax.axis_index("tp")
@@ -183,7 +200,7 @@
         ],
         axis=1,
     )
-    qkv_weight = lax.all_gather(qkv_own, "fsdp", axis=0, tiled=True)
+    qkv_weight = expand_the_circles(qkv_own)
     out_own = lax.dynamic_slice_in_dim(output_weight, ctx * q_cols, q_cols, 0).T
     out_weight = lax.all_gather(out_own, "fsdp", axis=0, tiled=True)
     gains = lax.all_gather(

time: 1160 us -> 1200 us (1.034)
  waiting for transfers between devices: 571 us -> 596 us
  blocking collectives: 122 us -> 137 us
    ppermute x0 -> x7, waiting for transfers between devices: none -> 100 us  [turns_detail(): latest = lax.ppermute(carry_in[0], axis_name=peer_axis, perm=row_list)]
    all_gather x1 -> x0, waiting for transfers between devices: 40 us -> none  [local(): qkv_weight = lax.all_gather(qkv_own, 'fsdp', axis=0, tiled=True)]
    all_gather x1, waiting for transfers between devices: 37.8 us -> 0.02 us  [local(): out_weight = lax.all_gather(out_own, 'fsdp', axis=0, tiled=True)]
    all_gather x1, blocking collectives: 31.4 us -> 53.3 us  [local(): lax.all_gather(jnp.concatenate([gain_attn_in, gain_attn_out, gain_ffn_in,...]
    unnamed x207 -> x225, local copies, waits for them, and re-layouts: 58.9 us -> 65.4 us
  transfers between devices with their start and end apart: 73 -> 79, of which waited for: 48 -> 51; matrix products, arithmetic and copies ran while one was open for 16% -> 15% of each run, Pallas kernels for 0% -> 0%
where the time goes in v1:
time: 1200 us
  waiting for transfers between devices  596 us (50%)
  local copies, waits for them, and re-layouts  166 us (14%)
  blocking collectives  137 us (11%)
  matrix products  128 us (11%)
  other arithmetic  79 us (7%)
  starting transfers between devices  73.1 us (6%)
  between operations  17 us (1%)
    ppermute x42, waiting for transfers between devices, hop(): return lax.ppermute(piece, 'fsdp', [(d, d ^ step) for d in range(n)])  339 us
    ppermute x28, waiting for transfers between devices, swap(): return lax.ppermute(piece, axis, [(0, 1), (1, 0)])  156 us
    dot_general x17, matrix products, dot(): lax.dot_general(lhs, rhs, (dims, ((), ())), preferred_element_type=f32)  121 us
    ppermute x7, waiting for transfers between devices, turns_detail(): latest = lax.ppermute(carry_in[0], axis_name=peer_axis, perm=row_list)  100 us
    unnamed x1, blocking collectives  83.3 us
    unnamed x225, local copies, waits for them, and re-layouts  65.4 us
    all_gather x1, blocking collectives, local(): lax.all_gather(jnp.concatenate([gain_attn_in, gain_attn_out, gain_ffn_in,...  53.3 us
    ppermute x42, starting transfers between devices, hop(): return lax.ppermute(piece, 'fsdp', [(d, d ^ step) for d in range(n)])  52.5 us
  transfers between devices with their start and end apart: 79, of which 51 were waited for; matrix products, arithmetic and copies ran while one was open for 15% of the time, Pallas kernels for 0%

profile of v1, /device:TPU:0, one launch (start us, length us, event | category | flops | bytes accessed | tf_op | source)
XLA Modules:
  0.0 1195.2 jit_solution(10672512387005342821)
XLA Ops:
  12.4 16.4 %collective-permute-done.2 = bf16[288,1024]{1,0:T(8,128)(2,1)S(1)} collective-permute-done((bf16[288,1024]{1,0:T(8,128)(2,1)S(1)}, bf16[288,1024]{1,0:T(8,128)(2,1)S(1)}, u32[]{:S(2)}, u32[]{:S(2)}) %collective-permute-start.2) | collective-permute-done | bytes 589856 | tf_op jit(solution)/shard_map/ppermute | solution.py:149
  28.8 17.2 %collective-permute-done.3 = bf16[288,1024]{1,0:T(8,128)(2,1)S(1)} collective-permute-done((bf16[288,1024]{1,0:T(8,128)(2,1)S(1)}, bf16[288,1024]{1,0:T(8,128)(2,1)S(1)}, u32[]{:S(2)}, u32[]{:S(2)}) %collective-permute-start.3) | collective-permute-done | bytes 589856 | tf_op jit(solution)/shard_map/ppermute | solution.py:149
  50.0 12.4 %collective-permute-done.4 = bf16[288,1024]{1,0:T(8,128)(2,1)S(1)} collective-permute-done((bf16[288,1024]{1,0:T(8,128)(2,1)S(1)}, bf16[288,1024]{1,0:T(8,128)(2,1)S(1)}, u32[]{:S(2)}, u32[]{:S(2)}) %collective-permute-start.4) | collective-permute-done | bytes 589856 | tf_op jit(solution)/shard_map/ppermute | solution.py:149
  62.6 23.8 %collective-permute-done.5 = bf16[288,1024]{1,0:T(8,128)(2,1)S(1)} collective-permute-done((bf16[288,1024]{1,0:T(8,128)(2,1)S(1)}, bf16[288,1024]{1,0:T(8,128)(2,1)S(1)}, u32[]{:S(2)}, u32[]{:S(2)}) %collective-permute-start.5) | collective-permute-done | bytes 589856 | tf_op jit(solution)/shard_map/ppermute | solution.py:149
  87.2 53.3 %all-gather = f32[8,1,1152]{2,1,0:T(1,128)S(1)} all-gather(f32[1,1,1152]{2,1,0:T(1,128)S(1)} %bitcast_convert_fusion.2), channel_id=1, replica_groups=mesh['fsdp'=8,'ctx'=2,'tp'=2] {'fsdp'}, dimensions={0}, use_global_device_ids=true | all-gather | bytes 41472 | tf_op jit(solution)/shard_map/all_gather | solution.py:206
  144.0 15.8 %collective-permute-done.7 = bf16[288,1024]{1,0:T(8,128)(2,1)} collective-permute-done((bf16[288,1024]{1,0:T(8,128)(2,1)}, bf16[288,1024]{1,0:T(8,128)(2,1)}, u32[]{:S(2)}, u32[]{:S(2)}) %collective-permute-start.7) | collective-permute-done | bytes 589856 | tf_op jit(solution)/shard_map/ppermute | solution.py:149
  162.7 14.8 %collective-permute-done.8 = bf16[288,1024]{1,0:T(8,128)(2,1)S(1)} collective-permute-done((bf16[288,1024]{1,0:T(8,128)(2,1)}, bf16[288,1024]{1,0:T(8,128)(2,1)S(1)}, u32[]{:S(2)}, u32[]{:S(2)}) %collective-permute-start.8) | collective-permute-done | bytes 589856 | tf_op jit(solution)/shard_map/ppermute | solution.py:149
  235.1 10.6 constant_dynamic-slice_fusion
  255.7 22.0 %collective-permute-done.12 = bf16[112,2304]{1,0:T(8,128)(2,1)S(1)} collective-permute-done((bf16[112,2304]{1,0:T(8,128)(2,1)S(1)}, bf16[112,2304]{1,0:T(8,128)(2,1)S(1)}, u32[]{:S(2)}, u32[]{:S(2)}) %collective-permute-start.12) | collective-permute-done | bytes 516128 | tf_op jit(solution)/shard_map/ppermute | solution.py:74
  317.1 20.4 %collective-permute-done.17 = bf16[112,2304]{1,0:T(8,128)(2,1)S(1)} collective-permute-done((bf16[112,2304]{1,0:T(8,128)(2,1)S(1)}, bf16[112,2304]{1,0:T(8,128)(2,1)S(1)}, u32[]{:S(2)}, u32[]{:S(2)}) %collective-permute-start.17) | collective-permute-done | bytes 516128 | tf_op jit(solution)/shard_map/ppermute | solution.py:74
  369.0 37.5 %collective-permute-done.26 = bf16[3,144,576]{2,1,0:T(8,128)(2,1)S(1)} collective-permute-done((bf16[3,144,576]{2,1,0:T(8,128)(2,1)}, bf16[3,144,576]{2,1,0:T(8,128)(2,1)S(1)}, u32[]{:S(2)}, u32[]{:S(2)}) %collective-permute-start.26) | collective-permute-done | bytes 497696 | tf_op jit(solution)/shard_map/ppermute | solution.py:74
  413.0 18.1 %collective-permute-done.28 = bf16[3,144,576]{2,1,0:T(8,128)(2,1)S(1)} collective-permute-done((bf16[3,144,576]{2,1,0:T(8,128)(2,1)}, bf16[3,144,576]{2,1,0:T(8,128)(2,1)S(1)}, u32[]{:S(2)}, u32[]{:S(2)}) %collective-permute-start.28) | collective-permute-done | bytes 497696 | tf_op jit(solution)/shard_map/ppermute | solution.py:74
  484.3 11.5 fusion.196
  495.8 14.4 %multiply_convert_fusion.1 = (bf16[1792,576]{0,1:T(8,128)(2,1)}, f32[1792,576]{0,1:T(8,128)}) fusion(f32[1792,576]{0,1:T(8,128)} %fusion.196, bf16[1792,2304]{1,0:T(8,128)(2,1)} %copy-done.58, bf16[2304,576]{1,0:T(8,128)(2,1)} %bitcast.52), kind=kOutput, calls=%fused_computation.24 | convolution fusion | flops 4766662656 | bytes 21233664 | tf_op jit(solution)/shard_map/dot_general | solution.py:66
  549.3 12.0 %collective-permute-done.39 = bf16[112,2304]{1,0:T(8,128)(2,1)S(1)} collective-permute-done((bf16[112,2304]{1,0:T(8,128)(2,1)S(1)}, bf16[112,2304]{1,0:T(8,128)(2,1)S(1)}, u32[]{:S(2)}, u32[]{:S(2)}) %collective-permute-start.39) | collective-permute-done | bytes 516128 | tf_op jit(solution)/shard_map/ppermute | solution.py:74
  572.4 11.1 collective-permute-done.38
  593.8 15.4 %collective-permute-done.37 = bf16[112,2304]{1,0:T(8,128)(2,1)S(1)} collective-permute-done((bf16[112,2304]{1,0:T(8,128)(2,1)}, bf16[112,2304]{1,0:T(8,128)(2,1)S(1)}, u32[]{:S(2)}, u32[]{:S(2)}) %collective-permute-start.37) | collective-permute-done | bytes 516128 | tf_op jit(solution)/shard_map/ppermute | solution.py:74
  618.6 19.6 %collective-permute-done.43 = bf16[112,2304]{1,0:T(8,128)(2,1)S(1)} collective-permute-done((bf16[112,2304]{1,0:T(8,128)(2,1)S(1)}, bf16[112,2304]{1,0:T(8,128)(2,1)S(1)}, u32[]{:S(2)}, u32[]{:S(2)}) %collective-permute-start.43) | collective-permute-done | bytes 516128 | tf_op jit(solution)/shard_map/ppermute | solution.py:74
  640.3 11.5 collective-permute-done.45
  652.8 11.0 collective-permute-done.48
  687.2 12.4 %fusion.7 = (bf16[1792,576]{0,1:T(8,128)(2,1)S(1)}, bf16[1792,576]{0,1:T(8,128)(2,1)S(1)}) fusion(f32[1792,576]{0,1:T(8,128)S(1)} %copy-done.82, f32[1792,576]{0,1:T(8,128)} %get-tuple-element.226, bf16[1792,2304]{1,0:T(8,128)(2,1)} %copy-done.56, bf16[2304,576]{1,0:T(8,128)(2,1)S(1)} %bitcast.453), kind=kOutput, calls=%fused_computation.20 | convolution fusion | flops 4785242112 | bytes 23298048 | tf_op jit(solution)/shard_map/dot_general | solution.py:66
  699.6 13.6 %fusion.198 = f32[1792,2304]{1,0:T(8,128)} fusion(bf16[1792,576]{0,1:T(8,128)(2,1)S(1)} %get-tuple-element.63, bf16[2304,576]{1,0:T(8,128)(2,1)} %bitcast.52), kind=kOutput, calls=%fused_computation.478 | convolution fusion | flops 4756340736 | bytes 21233664 | tf_op jit(solution)/shard_map/dot_general | solution.py:66
  713.2 15.1 %convolution_add_fusion = f32[1792,2304]{1,0:T(8,128)} fusion(f32[1792,2304]{1,0:T(8,128)} %fusion.198, bf16[1792,576]{0,1:T(8,128)(2,1)S(1)} %get-tuple-element.62, bf16[2304,576]{1,0:T(8,128)(2,1)} %bitcast.35), kind=kOutput, calls=%fused_computation | convolution fusion | flops 4760469504 | bytes 37748736 | tf_op jit(solution)/shard_map/dot_general | solution.py:66
  753.8 12.0 %collective-permute-done.56 = bf16[112,2304]{1,0:T(8,128)(2,1)S(1)} collective-permute-done((bf16[112,2304]{1,0:T(8,128)(2,1)S(1)}, bf16[112,2304]{1,0:T(8,128)(2,1)S(1)}, u32[]{:S(2)}, u32[]{:S(2)}) %collective-permute-start.56) | collective-permute-done | bytes 516128 | tf_op jit(solution)/shard_map/ppermute | solution.py:74
  776.9 11.1 collective-permute-done.55
  798.2 14.0 %collective-permute-done.54 = bf16[112,2304]{1,0:T(8,128)(2,1)S(1)} collective-permute-done((bf16[112,2304]{1,0:T(8,128)(2,1)S(1)}, bf16[112,2304]{1,0:T(8,128)(2,1)S(1)}, u32[]{:S(2)}, u32[]{:S(2)}) %collective-permute-start.54) | collective-permute-done | bytes 516128 | tf_op jit(solution)/shard_map/ppermute | solution.py:74
  911.4 28.8 %collective-permute-done.67 = bf16[8,144,576]{2,1,0:T(8,128)(2,1)} collective-permute-done((bf16[8,144,576]{2,1,0:T(8,128)(2,1)}, bf16[8,144,576]{2,1,0:T(8,128)(2,1)}, u32[]{:S(2)}, u32[]{:S(2)}) %collective-permute-start.67) | collective-permute-done | bytes 1327136 | tf_op jit(solution)/shard_map/ppermute | solution.py:70
  942.9 28.1 %collective-permute-done.68 = bf16[8,144,576]{2,1,0:T(8,128)(2,1)} collective-permute-done((bf16[8,144,576]{2,1,0:T(8,128)(2,1)}, bf16[8,144,576]{2,1,0:T(8,128)(2,1)}, u32[]{:S(2)}, u32[]{:S(2)}) %collective-permute-start.68) | collective-permute-done | bytes 1327136 | tf_op jit(solution)/shard_map/ppermute | solution.py:70
  1005.5 16.2 %collective-permute-done.70 = bf16[3,144,576]{2,1,0:T(8,128)(2,1)S(1)} collective-permute-done((bf16[3,144,576]{2,1,0:T(8,128)(2,1)S(1)}, bf16[3,144,576]{2,1,0:T(8,128)(2,1)S(1)}, u32[]{:S(2)}, u32[]{:S(2)}) %collective-permute-start.70) | collective-permute-done | bytes 497696 | tf_op jit(solution)/shard_map/ppermute | solution.py:74
  1023.2 10.9 collective-permute-done.71
  1037.4 22.8 %collective-permute-done.73 = bf16[3,144,576]{2,1,0:T(8,128)(2,1)S(1)} collective-permute-done((bf16[3,144,576]{2,1,0:T(8,128)(2,1)S(1)}, bf16[3,144,576]{2,1,0:T(8,128)(2,1)S(1)}, u32[]{:S(2)}, u32[]{:S(2)}) %collective-permute-start.73) | collective-permute-done | bytes 497696 | tf_op jit(solution)/shard_map/ppermute | solution.py:74
  1090.3 83.3 %all-reduce = f32[16,576]{1,0:T(8,128)S(1)} all-reduce(f32[16,576]{1,0:T(8,128)S(1)} %add.577), channel_id=3, replica_groups=mesh['fsdp'=8,'ctx'=2,'tp'=2] {'fsdp','ctx'}, use_global_device_ids=true, to_apply=%region_17.18.clone | all-reduce | flops 9216 | bytes 73728
  (534 shorter events, 541.2 us)
Async XLA Ops:
  7.3 188.4 %all-gather.3.cloned.1.call-start = ((), (), s32[]{:S(2)}) async-start(), calls=%async_computation.1 | async-start | bytes 2654208 | tf_op jit(solution)/shard_map/all_gather | solution.py:205
  47.8 93.1 %collective-permute-start = (bf16[112,2304]{1,0:T(8,128)(2,1)}, bf16[112,2304]{1,0:T(8,128)(2,1)}, u32[]{:S(2)}, u32[]{:S(2)}) collective-permute-start(bf16[112,2304]{1,0:T(8,128)(2,1)} %constant_dynamic-slice_fusion.11), channel_id=1, source_target_pairs={{0,2},{2,0},{1,3},{3,1},{4,6},{6,4},{5,7},{7,5},{8,10},{10,8},{9,1... | collective-permute-start | bytes 1548296 | tf_op jit(solution)/shard_map/ppermute | solution.py:70
  49.9 1125.0 %reduce-scatter.4.cloned.1.call-start = ((), (), s32[]{:S(2)}) async-start(), calls=%async_computation.2 | async-start | bytes 7962624 | tf_op jit(solution)/shard_map/reduce_scatter | solution.py:322
  86.4 54.6 %collective-permute-start.6 = (bf16[288,1024]{1,0:T(8,128)(2,1)S(1)}, bf16[288,1024]{1,0:T(8,128)(2,1)}, u32[]{:S(2)}, u32[]{:S(2)}) collective-permute-start(bf16[288,1024]{1,0:T(8,128)(2,1)S(1)} %collective-permute-done.5), channel_id=1, source_target_pairs={{0,4},{4,8},{8,12},{12,16},{16,20},{20,24},{24,28},{28,0},{1,5},{5... | collective-permute-start | bytes 1769480 | tf_op jit(solution)/shard_map/ppermute | solution.py:149
  245.8 111.3 %collective-permute-start.19 = (bf16[3,144,576]{2,1,0:T(8,128)(2,1)S(1)}, bf16[3,144,576]{2,1,0:T(8,128)(2,1)}, u32[]{:S(2)}, u32[]{:S(2)}) collective-permute-start(bf16[3,144,576]{2,1,0:T(8,128)(2,1)S(1)} %bitcast.455), channel_id=1, source_target_pairs={{0,2},{2,0},{1,3},{3,1},{4,6},{6,4},{5,7},{7,5},{8,10},{10,8},{9,1... | collective-permute-start | bytes 1493000 | tf_op jit(solution)/shard_map/ppermute | solution.py:70
  247.4 97.3 %collective-permute-start.20 = (bf16[3,144,576]{2,1,0:T(8,128)(2,1)S(1)}, bf16[3,144,576]{2,1,0:T(8,128)(2,1)}, u32[]{:S(2)}, u32[]{:S(2)}) collective-permute-start(bf16[3,144,576]{2,1,0:T(8,128)(2,1)S(1)} %bitcast.464), channel_id=1, source_target_pairs={{0,4},{4,0},{8,12},{12,8},{16,20},{20,16},{24,28},{28,24},{1,5},{5... | collective-permute-start | bytes 1493000 | tf_op jit(solution)/shard_map/ppermute | solution.py:74
  248.3 108.8 %collective-permute-start.22 = (bf16[3,144,576]{2,1,0:T(8,128)(2,1)}, bf16[3,144,576]{2,1,0:T(8,128)(2,1)}, u32[]{:S(2)}, u32[]{:S(2)}) collective-permute-start(bf16[3,144,576]{2,1,0:T(8,128)(2,1)} %bitcast.436), channel_id=1, source_target_pairs={{0,8},{4,12},{8,0},{12,4},{16,24},{20,28},{24,16},{28,20},{1,9},{5... | collective-permute-start | bytes 1493000 | tf_op jit(solution)/shard_map/ppermute | solution.py:74
  254.8 33.9 %collective-permute-start.13 = (bf16[112,2304]{1,0:T(8,128)(2,1)S(1)}, bf16[112,2304]{1,0:T(8,128)(2,1)S(1)}, u32[]{:S(2)}, u32[]{:S(2)}) collective-permute-start(bf16[112,2304]{1,0:T(8,128)(2,1)S(1)} %collective-permute-done.11), channel_id=1, source_target_pairs={{0,8},{4,12},{8,0},{12,4},{16,24},{20,28},{24,16},{28,20},{1,9},{5... | collective-permute-start | bytes 1548296 | tf_op jit(solution)/shard_map/ppermute | solution.py:74
  304.1 33.3 %collective-permute-start.17 = (bf16[112,2304]{1,0:T(8,128)(2,1)S(1)}, bf16[112,2304]{1,0:T(8,128)(2,1)S(1)}, u32[]{:S(2)}, u32[]{:S(2)}) collective-permute-start(bf16[112,2304]{1,0:T(8,128)(2,1)S(1)} %collective-permute-done.13), channel_id=1, source_target_pairs={{0,4},{4,0},{8,12},{12,8},{16,20},{20,16},{24,28},{28,24},{1,5},{5... | collective-permute-start | bytes 1548296 | tf_op jit(solution)/shard_map/ppermute | solution.py:74
  315.2 52.6 %collective-permute-start.24 = (bf16[3,144,576]{2,1,0:T(8,128)(2,1)S(1)}, bf16[3,144,576]{2,1,0:T(8,128)(2,1)}, u32[]{:S(2)}, u32[]{:S(2)}) collective-permute-start(bf16[3,144,576]{2,1,0:T(8,128)(2,1)S(1)} %bitcast.463), channel_id=1, source_target_pairs={{0,12},{4,8},{8,4},{12,0},{16,28},{20,24},{24,20},{28,16},{1,13},{... | collective-permute-start | bytes 1493000 | tf_op jit(solution)/shard_map/ppermute | solution.py:74
  338.3 143.5 %collective-permute-start.18 = (bf16[896,2304]{1,0:T(8,128)(2,1)}, bf16[896,2304]{1,0:T(8,128)(2,1)}, u32[]{:S(2)}, u32[]{:S(2)}) collective-permute-start(bf16[896,2304]{1,0:T(8,128)(2,1)} %get-tuple-element.191), channel_id=1, source_target_pairs={{0,1},{1,0},{2,3},{3,2},{4,5},{5,4},{6,7},{7,6},{8,9},{9,8},{10,11... | collective-permute-start | bytes 12386312 | tf_op jit(solution)/shard_map/ppermute | solution.py:70
  357.1 49.4 %collective-permute-start.26 = (bf16[3,144,576]{2,1,0:T(8,128)(2,1)}, bf16[3,144,576]{2,1,0:T(8,128)(2,1)S(1)}, u32[]{:S(2)}, u32[]{:S(2)}) collective-permute-start(bf16[3,144,576]{2,1,0:T(8,128)(2,1)} %bitcast.468), channel_id=1, source_target_pairs={{0,16},{4,20},{8,24},{12,28},{16,0},{20,4},{24,8},{28,12},{1,17},{... | collective-permute-start | bytes 1493000 | tf_op jit(solution)/shard_map/ppermute | solution.py:74
  357.2 52.4 %collective-permute-start.23 = (bf16[3,144,576]{2,1,0:T(8,128)(2,1)}, bf16[3,144,576]{2,1,0:T(8,128)(2,1)S(1)}, u32[]{:S(2)}, u32[]{:S(2)}) collective-permute-start(bf16[3,144,576]{2,1,0:T(8,128)(2,1)} %collective-permute-done.22), channel_id=1, source_target_pairs={{0,2},{2,0},{1,3},{3,1},{4,6},{6,4},{5,7},{7,5},{8,10},{10,8},{9,1... | collective-permute-start | bytes 1493000 | tf_op jit(solution)/shard_map/ppermute | solution.py:70
  361.9 69.2 %collective-permute-start.28 = (bf16[3,144,576]{2,1,0:T(8,128)(2,1)}, bf16[3,144,576]{2,1,0:T(8,128)(2,1)S(1)}, u32[]{:S(2)}, u32[]{:S(2)}) collective-permute-start(bf16[3,144,576]{2,1,0:T(8,128)(2,1)} %bitcast.467), channel_id=1, source_target_pairs={{0,20},{4,16},{8,28},{12,24},{16,4},{20,0},{24,12},{28,8},{1,21},{... | collective-permute-start | bytes 1493000 | tf_op jit(solution)/shard_map/ppermute | solution.py:74
  367.8 65.8 %collective-permute-start.30 = (bf16[3,144,576]{2,1,0:T(8,128)(2,1)S(1)}, bf16[3,144,576]{2,1,0:T(8,128)(2,1)S(1)}, u32[]{:S(2)}, u32[]{:S(2)}) collective-permute-start(bf16[3,144,576]{2,1,0:T(8,128)(2,1)S(1)} %bitcast.466), channel_id=1, source_target_pairs={{0,24},{4,28},{8,16},{12,20},{16,8},{20,12},{24,0},{28,4},{1,25},{... | collective-permute-start | bytes 1493000 | tf_op jit(solution)/shard_map/ppermute | solution.py:74
  435.1 35.2 %collective-permute-start.31 = (bf16[3,144,576]{2,1,0:T(8,128)(2,1)S(1)}, bf16[3,144,576]{2,1,0:T(8,128)(2,1)S(1)}, u32[]{:S(2)}, u32[]{:S(2)}) collective-permute-start(bf16[3,144,576]{2,1,0:T(8,128)(2,1)S(1)} %collective-permute-done.30), channel_id=1, source_target_pairs={{0,2},{2,0},{1,3},{3,1},{4,6},{6,4},{5,7},{7,5},{8,10},{10,8},{9,1... | collective-permute-start | bytes 1493000 | tf_op jit(solution)/shard_map/ppermute | solution.py:70
  435.6 45.4 %collective-permute-start.33 = (bf16[3,144,576]{2,1,0:T(8,128)(2,1)S(1)}, bf16[3,144,576]{2,1,0:T(8,128)(2,1)S(1)}, u32[]{:S(2)}, u32[]{:S(2)}) collective-permute-start(bf16[3,144,576]{2,1,0:T(8,128)(2,1)S(1)} %collective-permute-done.32), channel_id=1, source_target_pairs={{0,2},{2,0},{1,3},{3,1},{4,6},{6,4},{5,7},{7,5},{8,10},{10,8},{9,1... | collective-permute-start | bytes 1493000 | tf_op jit(solution)/shard_map/ppermute | solution.py:70
  548.7 34.7 %collective-permute-start.38 = (bf16[112,2304]{1,0:T(8,128)(2,1)S(1)}, bf16[112,2304]{1,0:T(8,128)(2,1)S(1)}, u32[]{:S(2)}, u32[]{:S(2)}) collective-permute-start(bf16[112,2304]{1,0:T(8,128)(2,1)S(1)} %get-tuple-element.82), channel_id=1, source_target_pairs={{0,4},{4,0},{8,12},{12,8},{16,20},{20,16},{24,28},{28,24},{1,5},{5... | collective-permute-start | bytes 1548296 | tf_op jit(solution)/shard_map/ppermute | solution.py:74
  617.9 34.5 %collective-permute-start.46 = (bf16[112,2304]{1,0:T(8,128)(2,1)S(1)}, bf16[112,2304]{1,0:T(8,128)(2,1)S(1)}, u32[]{:S(2)}, u32[]{:S(2)}) collective-permute-start(bf16[112,2304]{1,0:T(8,128)(2,1)S(1)} %get-tuple-element.37), channel_id=1, source_target_pairs={{0,4},{4,0},{8,12},{12,8},{16,20},{20,16},{24,28},{28,24},{1,5},{5... | collective-permute-start | bytes 1548296 | tf_op jit(solution)/shard_map/ppermute | solution.py:74
  753.2 34.7 %collective-permute-start.55 = (bf16[112,2304]{1,0:T(8,128)(2,1)S(1)}, bf16[112,2304]{1,0:T(8,128)(2,1)S(1)}, u32[]{:S(2)}, u32[]{:S(2)}) collective-permute-start(bf16[112,2304]{1,0:T(8,128)(2,1)S(1)} %get-tuple-element.78), channel_id=1, source_target_pairs={{0,4},{4,0},{8,12},{12,8},{16,20},{20,16},{24,28},{28,24},{1,5},{5... | collective-permute-start | bytes 1548296 | tf_op jit(solution)/shard_map/ppermute | solution.py:74
  873.4 35.2 %collective-permute-start.66 = (bf16[8,144,576]{2,1,0:T(8,128)(2,1)S(1)}, bf16[8,144,576]{2,1,0:T(8,128)(2,1)}, u32[]{:S(2)}, u32[]{:S(2)}) collective-permute-start(bf16[8,144,576]{2,1,0:T(8,128)(2,1)S(1)} %fusion.28), channel_id=1, source_target_pairs={{0,2},{2,0},{1,3},{3,1},{4,6},{6,4},{5,7},{7,5},{8,10},{10,8},{9,1... | collective-permute-start | bytes 3981320 | tf_op jit(solution)/shard_map/ppermute | solution.py:70
  886.8 53.4 %collective-permute-start.67 = (bf16[8,144,576]{2,1,0:T(8,128)(2,1)}, bf16[8,144,576]{2,1,0:T(8,128)(2,1)}, u32[]{:S(2)}, u32[]{:S(2)}) collective-permute-start(bf16[8,144,576]{2,1,0:T(8,128)(2,1)} %fusion.29), channel_id=1, source_target_pairs={{0,2},{2,0},{1,3},{3,1},{4,6},{6,4},{5,7},{7,5},{8,10},{10,8},{9,1... | collective-permute-start | bytes 3981320 | tf_op jit(solution)/shard_map/ppermute | solution.py:70
  897.8 73.2 %collective-permute-start.68 = (bf16[8,144,576]{2,1,0:T(8,128)(2,1)}, bf16[8,144,576]{2,1,0:T(8,128)(2,1)}, u32[]{:S(2)}, u32[]{:S(2)}) collective-permute-start(bf16[8,144,576]{2,1,0:T(8,128)(2,1)} %fusion.30), channel_id=1, source_target_pairs={{0,2},{2,0},{1,3},{3,1},{4,6},{6,4},{5,7},{7,5},{8,10},{10,8},{9,1... | collective-permute-start | bytes 3981320 | tf_op jit(solution)/shard_map/ppermute | solution.py:70
  903.5 72.1 %collective-permute-start.61 = (f32[224,2304]{1,0:T(8,128)}, f32[224,2304]{1,0:T(8,128)}, u32[]{:S(2)}, u32[]{:S(2)}) collective-permute-start(f32[224,2304]{1,0:T(8,128)} %pad_maximum_fusion.4), channel_id=1, source_target_pairs={{0,1},{1,0},{2,3},{3,2},{4,5},{5,4},{6,7},{7,6},{8,9},{9,8},{10,11... | collective-permute-start | bytes 6193160 | tf_op jit(solution)/shard_map/ppermute | solution.py:70
  904.2 74.1 %collective-permute-start.42 = (bf16[112,2304]{1,0:T(8,128)(2,1)}, bf16[112,2304]{1,0:T(8,128)(2,1)S(1)}, u32[]{:S(2)}, u32[]{:S(2)}) collective-permute-start(bf16[112,2304]{1,0:T(8,128)(2,1)} %get-tuple-element.92), channel_id=1, source_target_pairs={{0,1},{1,0},{2,3},{3,2},{4,5},{5,4},{6,7},{7,6},{8,9},{9,8},{10,11... | collective-permute-start | bytes 1548296 | tf_op jit(solution)/shard_map/ppermute | solution.py:70
  980.9 40.9 %collective-permute-start.70 = (bf16[3,144,576]{2,1,0:T(8,128)(2,1)S(1)}, bf16[3,144,576]{2,1,0:T(8,128)(2,1)S(1)}, u32[]{:S(2)}, u32[]{:S(2)}) collective-permute-start(bf16[3,144,576]{2,1,0:T(8,128)(2,1)S(1)} %get-tuple-element.71), channel_id=1, source_target_pairs={{0,8},{4,12},{8,0},{12,4},{16,24},{20,28},{24,16},{28,20},{1,9},{5... | collective-permute-start | bytes 1493000 | tf_op jit(solution)/shard_map/ppermute | solution.py:74
  982.5 51.6 %collective-permute-start.71 = (bf16[3,144,576]{2,1,0:T(8,128)(2,1)S(1)}, bf16[3,144,576]{2,1,0:T(8,128)(2,1)S(1)}, u32[]{:S(2)}, u32[]{:S(2)}) collective-permute-start(bf16[3,144,576]{2,1,0:T(8,128)(2,1)S(1)} %get-tuple-element.70), channel_id=1, source_target_pairs={{0,12},{4,8},{8,4},{12,0},{16,28},{20,24},{24,20},{28,16},{1,13},{... | collective-permute-start | bytes 1493000 | tf_op jit(solution)/shard_map/ppermute | solution.py:74
  983.2 52.9 %collective-permute-start.72 = (bf16[3,144,576]{2,1,0:T(8,128)(2,1)S(1)}, bf16[3,144,576]{2,1,0:T(8,128)(2,1)S(1)}, u32[]{:S(2)}, u32[]{:S(2)}) collective-permute-start(bf16[3,144,576]{2,1,0:T(8,128)(2,1)S(1)} %get-tuple-element.69), channel_id=1, source_target_pairs={{0,16},{4,20},{8,24},{12,28},{16,0},{20,4},{24,8},{28,12},{1,17},{... | collective-permute-start | bytes 1493000 | tf_op jit(solution)/shard_map/ppermute | solution.py:74
  988.9 71.3 %collective-permute-start.73 = (bf16[3,144,576]{2,1,0:T(8,128)(2,1)S(1)}, bf16[3,144,576]{2,1,0:T(8,128)(2,1)S(1)}, u32[]{:S(2)}, u32[]{:S(2)}) collective-permute-start(bf16[3,144,576]{2,1,0:T(8,128)(2,1)S(1)} %get-tuple-element.68), channel_id=1, source_target_pairs={{0,20},{4,16},{8,28},{12,24},{16,4},{20,0},{24,12},{28,8},{1,21},{... | collective-permute-start | bytes 1493000 | tf_op jit(solution)/shard_map/ppermute | solution.py:74
  1001.6 58.6 %collective-permute-start.74 = (bf16[3,144,576]{2,1,0:T(8,128)(2,1)S(1)}, bf16[3,144,576]{2,1,0:T(8,128)(2,1)S(1)}, u32[]{:S(2)}, u32[]{:S(2)}) collective-permute-start(bf16[3,144,576]{2,1,0:T(8,128)(2,1)S(1)} %get-tuple-element.67), channel_id=1, source_target_pairs={{0,24},{4,28},{8,16},{12,20},{16,8},{20,12},{24,0},{28,4},{1,25},{... | collective-permute-start | bytes 1493000 | tf_op jit(solution)/shard_map/ppermute | solution.py:74
  1034.1 33.1 %collective-permute-start.75 = (bf16[3,144,576]{2,1,0:T(8,128)(2,1)}, bf16[3,144,576]{2,1,0:T(8,128)(2,1)}, u32[]{:S(2)}, u32[]{:S(2)}) collective-permute-start(bf16[3,144,576]{2,1,0:T(8,128)(2,1)} %get-tuple-element.66), channel_id=1, source_target_pairs={{0,28},{4,24},{8,20},{12,16},{16,12},{20,8},{24,4},{28,0},{1,29},{... | collective-permute-start | bytes 1493000 | tf_op jit(solution)/shard_map/ppermute | solution.py:74
  1037.4 138.8 %collective-permute-start.64 = (bf16[224,2304]{1,0:T(8,128)(2,1)}, bf16[224,2304]{1,0:T(8,128)(2,1)}, u32[]{:S(2)}, u32[]{:S(2)}) collective-permute-start(bf16[224,2304]{1,0:T(8,128)(2,1)} %pad_maximum_fusion.7), channel_id=1, source_target_pairs={{0,1},{1,0},{2,3},{3,2},{4,5},{5,4},{6,7},{7,6},{8,9},{9,8},{10,11... | collective-permute-start | bytes 3096584 | tf_op jit(solution)/shard_map/ppermute | solution.py:70
  (139 other events, 2604.7 us)
Sparse Core Ops, SparseCore 0:
  50.0 65.3 all-gather.2
  860.8 150.1 reduce-scatter.3
